TPU v7x, 32 devices: a whole 2x2x4 slice. The times are simulated.
32 devices in a mesh: dp: 4 (over z), expert: 8 (over y, x, core).
Axes of the slice: x: 2, y: 2, z: 4, core: 2. Of those that a mesh axis runs over, the one named last changes fastest.
Arguments:
- tokens: bfloat16 [4096, 2048], P(('dp', 'expert')), may hold values from -6 to 6
- expert_ids: int32 [4096, 1], P(('dp', 'expert')), may hold values from 0 to 7; in each aligned block of 128 rows (0 to 127, 128 to 255, ...) at most 32 rows name the same one
- route_weights: bfloat16 [4096, 1], P(('dp', 'expert')), may hold values from 0.099609375 to 1
- out_grad: bfloat16 [4096, 2048], P(('dp', 'expert')), may hold values from -6 to 6
- gate_weight: bfloat16 [8, 768, 2048], P('expert'), may hold values from -0.125 to 0.125
- down_weight: bfloat16 [8, 768, 2048], P('expert'), may hold values from -0.21875 to 0.21875
Outputs:
- token_grad: bfloat16 [4096, 2048], P(('dp', 'expert'))
- route_grad: bfloat16 [4096, 1], P(('dp', 'expert'))
- gate_grad: bfloat16 [8, 768, 2048], P('expert', 'dp')
- down_grad: bfloat16 [8, 768, 2048], P('expert', 'dp')
Inputs may be any that keep to these rules, and one draw needn't show every extreme that they name: `expert_ids`: the 1 expert of a token differ. Among the 128 tokens of one device no expert is named more than 32 times, a bound that some block reaches.
All inputs are finite; a program needn't handle non-finite values.
Results may differ from a plain program's by a relative error of at most 0.015.
Values may be sent and summed in bfloat16 or wider, within the bound.
A program may use at most 64 MiB of HBM per device.

v0:
```python
import jax
import jax.numpy as jnp
from jax import lax
from jax.sharding import PartitionSpec as P


def silu_slope(values):
    sigma = jax.nn.sigmoid(values)
    return sigma * (1.0 + values * (1.0 - sigma))


def contract_rows(left, right):
    return lax.dot_general(
        left, right, (((0,), (0,)), ((), ())), preferred_element_type=jnp.float32
    )


def sum_down(hidden, scaled):
    return lax.psum_scatter(
        contract_rows(hidden, scaled).astype(jnp.bfloat16), "dp", scatter_dimension=0, tiled=True
    ).astype(jnp.float32)


def per_device(tokens, expert_ids, route_weights, out_grad, gate_weight, down_weight):
    tok_rows, top = expert_ids.shape
    width = tokens.shape[1]
    experts = lax.axis_size("expert")
    capacity = max(2, 2 * tok_rows * top // experts)
    slots = experts * capacity
    routed = expert_ids.reshape(-1)
    one_hot = (routed[:, None] == jnp.arange(experts, dtype=jnp.int32)[None, :]).astype(jnp.int32)
    ranking = jnp.sum((jnp.cumsum(one_hot, axis=0) - 1) * one_hot, axis=1)
    targets = routed * capacity + ranking
    matches = (jnp.arange(slots, dtype=jnp.int32)[:, None] == targets[None, :]).astype(jnp.int32)
    filled = jnp.sum(matches, axis=1) > 0
    source_pair = jnp.sum(matches * jnp.arange(tok_rows * top, dtype=jnp.int32)[None, :], axis=1)
    source_token = source_pair // top
    nought = jnp.zeros((), jnp.bfloat16)
    sent = jnp.where(filled[:, None], tokens[source_token], nought).reshape(
        experts, capacity, width
    )
    arrived = lax.all_to_all(sent, "expert", split_axis=0, concat_axis=0, tiled=True)
    grads_sent = jnp.where(filled[:, None], out_grad[source_token], nought).reshape(
        experts, capacity, width
    )
    weights_sent = jnp.where(filled, route_weights.reshape(-1)[source_pair], nought).reshape(
        experts, capacity
    )
    grads_arrived, weights_arrived = (
        lax.all_to_all(grads_sent, "expert", split_axis=0, concat_axis=0, tiled=True),
        lax.all_to_all(weights_sent, "expert", split_axis=0, concat_axis=0, tiled=True),
    )
    inputs = arrived.reshape(slots, width)
    upstream = grads_arrived.reshape(slots, width)
    scales = weights_arrived.reshape(slots)
    gate = gate_weight[0]
    down = down_weight[0]
    preact = lax.dot_general(
        inputs, gate, (((1,), (1,)), ((), ())), preferred_element_type=jnp.float32
    )
    hidden = jax.nn.silu(preact).astype(jnp.bfloat16)
    outputs = jnp.dot(hidden, down, preferred_element_type=jnp.float32)
    prob_slots = jnp.sum(upstream.astype(jnp.float32) * outputs, axis=1).astype(jnp.bfloat16)
    scaled = (scales.astype(jnp.float32)[:, None] * upstream.astype(jnp.float32)).astype(
        jnp.bfloat16
    )
    hidden_grad = lax.dot_general(
        scaled, down, (((1,), (1,)), ((), ())), preferred_element_type=jnp.float32
    )
    pre_grad = (hidden_grad * silu_slope(preact)).astype(jnp.bfloat16)
    input_grad = jnp.dot(pre_grad, gate, preferred_element_type=jnp.float32).astype(jnp.bfloat16)
    gate_sum = lax.psum_scatter(
        contract_rows(pre_grad, inputs).astype(jnp.bfloat16), "dp", scatter_dimension=0, tiled=True
    )
    down_sum = sum_down(hidden, scaled)
    back_grad, back_prob = (
        lax.all_to_all(
            input_grad.reshape(experts, capacity, width),
            "expert",
            split_axis=0,
            concat_axis=0,
            tiled=True,
        ),
        lax.all_to_all(
            prob_slots.reshape(experts, capacity), "expert", split_axis=0, concat_axis=0, tiled=True
        ),
    )
    pair_grad = (
        back_grad.reshape(slots, width)[targets].astype(jnp.float32).reshape(tok_rows, top, width)
    )
    token_grad = jnp.sum(pair_grad, axis=1).astype(jnp.bfloat16)
    route_grad = back_prob.reshape(slots)[targets].reshape(tok_rows, top)
    gate_grad = gate_sum[None]
    down_grad = down_sum.astype(jnp.bfloat16)[None]
    return (token_grad, route_grad, gate_grad, down_grad)


def solution(mesh):
    placed = (
        P(("dp", "expert"), None),
        P(("dp", "expert"), None),
        P(("dp", "expert"), None),
        P(("dp", "expert"), None),
        P("expert", None, None),
        P("expert", None, None),
    )
    return jax.shard_map(
        per_device,
        mesh=mesh,
        in_specs=placed,
        out_specs=(
            P(("dp", "expert"), None),
            P(("dp", "expert"), None),
            P("expert", "dp", None),
            P("expert", "dp", None),
        ),
        check_vma=False,
    )
```

profile of v0, /device:TPU:1, one launch (start us, length us, event | category | flops | bytes accessed | tf_op | source)
XLA Modules:
  0.0 203.4 jit_solution(6789307509313201399)
XLA Ops:
  7.2 0.9 fusion.24
  8.1 0.2 reduce_window_sum.11
  8.2 0.8 select_reduce_fusion.1
  9.1 0.7 multiply_add_fusion
  9.7 0.2 convert_reduce_fusion
  9.9 1.9 gather_fusion
  11.8 0.7 select_n.54
  12.5 5.2 %all-to-all-start = ((bf16[8,1,32]{2,1,0:T(2,128)(2,1)}), bf16[8,1,32]{2,1,0:T(2,128)(2,1)S(1)}, u32[]{:S(2)}, u32[]{:S(2)}) async-start(bf16[8,1,32]{2,1,0:T(2,128)(2,1)} %select_n.54), calls=%async_computation | async-start | bytes 8192 | tf_op jit(solution)/shard_map/all_to_all | solution.py:51
  17.8 4.5 %gather_fusion.2 = bf16[256,2048]{1,0:T(8,128)(2,1)} fusion(bf16[128,2048]{1,0:T(8,128)(2,1)} %param.6, s32[1024]{0:T(1024)S(1)} %pad_clamp_fusion.1), kind=kCustom, calls=%fused_computation.2 | custom fusion | bytes 2098176 | tf_op jit(solution)/shard_map/gather | solution.py:39
  22.3 4.5 %gather_fusion.1 = bf16[256,2048]{1,0:T(8,128)(2,1)} fusion(bf16[128,2048]{1,0:T(8,128)(2,1)} %param.9, s32[1024]{0:T(1024)S(1)} %pad_clamp_fusion.1), kind=kCustom, calls=%fused_computation.1 | custom fusion | bytes 2098176 | tf_op jit(solution)/shard_map/gather | solution.py:43
  26.7 3.1 %broadcast_select_fusion = (bf16[8,32,2048]{2,1,0:T(8,128)(2,1)}, bf16[8,32,2048]{2,1,0:T(8,128)(2,1)}) fusion(bf16[8,32,2048]{2,1,0:T(8,128)(2,1)} %bitcast.53, pred[8,32]{1,0:T(8,128)(4,1)S(1)} %gt.20, bf16[8,32,2048]{2,1,0:T(8,128)(2,1)} %bitcast.54), kind=kLoop, calls=%fused_computation.23 | loop fusion | flops 1048576 | bytes 4194560 | tf_op jit(solution)/shard_map/jit(_where)/select_n | solution.py:39
  29.9 18.4 %all_to_all.27 = bf16[8,32,2048]{2,1,0:T(8,128)(2,1)} all-to-all(bf16[8,32,2048]{2,1,0:T(8,128)(2,1)} %get-tuple-element.8), channel_id=1, replica_groups=mesh['dp'=4,'expert'=8] {'expert'}, dimensions={0} | all-to-all | bytes 2097152 | tf_op jit(solution)/shard_map/all_to_all | solution.py:42
  48.3 5.3 %all-to-all-start.1 = ((bf16[8,32,2048]{2,1,0:T(8,128)(2,1)}), bf16[8,32,2048]{2,1,0:T(8,128)(2,1)}, u32[]{:S(2)}, u32[]{:S(2)}) async-start(bf16[8,32,2048]{2,1,0:T(8,128)(2,1)} %get-tuple-element.9), calls=%async_computation.1 | async-start | bytes 2097152 | tf_op jit(solution)/shard_map/all_to_all | solution.py:50
  53.7 3.1 %fusion.2 = f32[256,768]{1,0:T(8,128)} fusion(bf16[256,2048]{1,0:T(8,128)(2,1)} %bitcast.55, bf16[1,768,2048]{2,1,0:T(8,128)(2,1)S(1)} %copy-done), kind=kOutput, calls=%fused_computation.9 | convolution fusion | flops 805306368 | bytes 4980736 | tf_op jit(solution)/shard_map/dot_general | solution.py:58
  56.8 8.7 %all-to-all-done.1 = bf16[8,32,2048]{2,1,0:T(8,128)(2,1)} async-done(((bf16[8,32,2048]{2,1,0:T(8,128)(2,1)}), bf16[8,32,2048]{2,1,0:T(8,128)(2,1)}, u32[]{:S(2)}, u32[]{:S(2)}) %all-to-all-start.1) | async-done | bytes 1048608 | tf_op jit(solution)/shard_map/all_to_all | solution.py:50
  65.5 1.5 fusion.14
  67.0 3.9 %convolution_convert_fusion = bf16[768,2048]{1,0:T(8,128)(2,1)} fusion(bf16[256,2048]{1,0:T(8,128)(2,1)S(1)} %fusion.14, f32[256,768]{1,0:T(8,128)} %fusion.2), kind=kOutput, calls=%fused_computation.5 | convolution fusion | flops 807862272 | bytes 4980736 | tf_op jit(solution)/shard_map/dot_general | solution.py:13
  70.9 1.5 multiply_convert_fusion
  72.4 3.4 %fusion.21 = bf16[256,768]{1,0:T(8,128)(2,1)S(1)} fusion(bf16[256,2048]{1,0:T(8,128)(2,1)S(1)} %bitcast.58, bf16[1,768,2048]{2,1,0:T(8,128)(2,1)} %param.11, f32[256,768]{1,0:T(8,128)} %fusion.2), kind=kOutput, calls=%fused_computation.22 | convolution fusion | flops 807075840 | bytes 5373952 | tf_op jit(solution)/shard_map/dot_general | solution.py:67
  75.8 2.7 %convolution_convert_fusion.1 = bf16[768,2048]{1,0:T(8,128)(2,1)} fusion(bf16[256,768]{1,0:T(8,128)(2,1)S(1)} %fusion.21, bf16[256,2048]{1,0:T(8,128)(2,1)S(1)} %bitcast.56), kind=kOutput, calls=%fused_computation.6 | convolution fusion | flops 806879232 | bytes 4587520 | tf_op jit(solution)/shard_map/dot_general | solution.py:13
  78.5 4.1 %fusion.15 = bf16[256]{0:T(256)(128)(2,1)S(1)} fusion(bf16[1,768,2048]{2,1,0:T(8,128)(2,1)} %param.11, f32[256,768]{1,0:T(8,128)} %fusion.2, bf16[256,2048]{1,0:T(8,128)(2,1)} %bitcast.45), kind=kOutput, calls=%fused_computation.20 | convolution fusion | flops 807862016 | bytes 4981248 | tf_op jit(solution)/shard_map/dot_general | solution.py:62
  82.6 0.7 convert_element_type.97
  83.3 6.2 %all-to-all-start.4 = ((bf16[8,1,32]{2,1,0:T(2,128)(2,1)}), bf16[8,1,32]{2,1,0:T(2,128)(2,1)S(1)}, u32[]{:S(2)}, u32[]{:S(2)}) async-start(bf16[8,1,32]{2,1,0:T(2,128)(2,1)} %convert_element_type.97), calls=%async_computation.4 | async-start | bytes 8192 | tf_op jit(solution)/shard_map/all_to_all | solution.py:84
  89.5 2.0 fusion.11
  91.5 2.4 %all-to-all-done.4 = bf16[8,1,32]{2,1,0:T(2,128)(2,1)S(1)} async-done(((bf16[8,1,32]{2,1,0:T(2,128)(2,1)}), bf16[8,1,32]{2,1,0:T(2,128)(2,1)S(1)}, u32[]{:S(2)}, u32[]{:S(2)}) %all-to-all-start.4) | async-done | bytes 544 | tf_op jit(solution)/shard_map/all_to_all | solution.py:84
  93.9 4.4 %all-to-all-start.3 = ((bf16[8,32,2048]{2,1,0:T(8,128)(2,1)}), bf16[8,32,2048]{2,1,0:T(8,128)(2,1)}, u32[]{:S(2)}, u32[]{:S(2)}) async-start(bf16[8,32,2048]{2,1,0:T(8,128)(2,1)} %bitcast.57), calls=%async_computation.3 | async-start | bytes 2097152 | tf_op jit(solution)/shard_map/all_to_all | solution.py:77
  98.3 0.1 reshape.150
  98.4 1.7 gather_fusion.4
  100.2 10.0 %all-to-all-done.3 = bf16[8,32,2048]{2,1,0:T(8,128)(2,1)} async-done(((bf16[8,32,2048]{2,1,0:T(8,128)(2,1)}), bf16[8,32,2048]{2,1,0:T(8,128)(2,1)}, u32[]{:S(2)}, u32[]{:S(2)}) %all-to-all-start.3) | async-done | bytes 1048608 | tf_op jit(solution)/shard_map/all_to_all | solution.py:77
  110.2 3.6 %gather_fusion.3 = bf16[128,2048]{1,0:T(8,128)(2,1)} fusion(bf16[256,2048]{1,0:T(8,128)(2,1)} %bitcast.12, s32[1024]{0:T(1024)S(1)} %pad_clamp_fusion), kind=kCustom, calls=%fused_computation.3 | custom fusion | bytes 1049088 | tf_op jit(solution)/shard_map/gather | solution.py:89
  113.8 19.6 %reduce-scatter.5.cloned.1.call-done = bf16[192,2048]{1,0:T(8,128)(2,1)} async-done(((bf16[768,2048]{1,0:T(8,128)(2,1)}), bf16[192,2048]{1,0:T(8,128)(2,1)}) %reduce-scatter.5.cloned.1.call-update) | async-done | bytes 786448 | tf_op jit(solution)/shard_map/reduce_scatter | solution.py:19
  133.4 63.2 %reduce-scatter.3.cloned.1.call-done = bf16[192,2048]{1,0:T(8,128)(2,1)} async-done(((bf16[768,2048]{1,0:T(8,128)(2,1)}), bf16[192,2048]{1,0:T(8,128)(2,1)}) %reduce-scatter.3.cloned.1.call-update) | async-done | bytes 786448 | tf_op jit(solution)/shard_map/reduce_scatter | solution.py:72
  (21 shorter events, 0.3 us)
Async XLA Ops:
  7.2 46.5 %copy-start = (bf16[1,768,2048]{2,1,0:T(8,128)(2,1)S(1)}, bf16[1,768,2048]{2,1,0:T(8,128)(2,1)}, u32[]{:S(2)}) copy-start(bf16[1,768,2048]{2,1,0:T(8,128)(2,1)} %param.10) | copy-start | bytes 9437188
  12.5 17.3 %all-to-all-start = ((bf16[8,1,32]{2,1,0:T(2,128)(2,1)}), bf16[8,1,32]{2,1,0:T(2,128)(2,1)S(1)}, u32[]{:S(2)}, u32[]{:S(2)}) async-start(bf16[8,1,32]{2,1,0:T(2,128)(2,1)} %select_n.54), calls=%async_computation | async-start | bytes 8192 | tf_op jit(solution)/shard_map/all_to_all | solution.py:51
  48.3 17.2 %all-to-all-start.1 = ((bf16[8,32,2048]{2,1,0:T(8,128)(2,1)}), bf16[8,32,2048]{2,1,0:T(8,128)(2,1)}, u32[]{:S(2)}, u32[]{:S(2)}) async-start(bf16[8,32,2048]{2,1,0:T(8,128)(2,1)} %get-tuple-element.9), calls=%async_computation.1 | async-start | bytes 2097152 | tf_op jit(solution)/shard_map/all_to_all | solution.py:50
  53.6 79.8 %reduce-scatter.5.cloned.1.call-start = ((), (), s32[]{:S(2)}) async-start(), calls=%async_computation.8 | async-start | bytes 3932160 | tf_op jit(solution)/shard_map/reduce_scatter | solution.py:19
  70.9 125.7 %reduce-scatter.3.cloned.1.call-start = ((), (), s32[]{:S(2)}) async-start(), calls=%async_computation.7 | async-start | bytes 3932160 | tf_op jit(solution)/shard_map/reduce_scatter | solution.py:72
  72.4 3.4 %copy-start.1 = (bf16[8,32,2048]{2,1,0:T(8,128)(2,1)S(1)}, bf16[8,32,2048]{2,1,0:T(8,128)(2,1)}, u32[]{:S(2)}) copy-start(bf16[8,32,2048]{2,1,0:T(8,128)(2,1)} %all_to_all.27) | copy-start | bytes 3145732
  83.3 10.6 %all-to-all-start.4 = ((bf16[8,1,32]{2,1,0:T(2,128)(2,1)}), bf16[8,1,32]{2,1,0:T(2,128)(2,1)S(1)}, u32[]{:S(2)}, u32[]{:S(2)}) async-start(bf16[8,1,32]{2,1,0:T(2,128)(2,1)} %convert_element_type.97), calls=%async_computation.4 | async-start | bytes 8192 | tf_op jit(solution)/shard_map/all_to_all | solution.py:84
  89.5 8.8 %copy-start.2 = (s32[128,1]{0,1:T(1,128)S(1)}, s32[128,1]{0,1:T(1,128)}, u32[]{:S(2)}) copy-start(s32[128,1]{0,1:T(1,128)} %param.7) | copy-start | bytes 1540
  93.9 16.3 %all-to-all-start.3 = ((bf16[8,32,2048]{2,1,0:T(8,128)(2,1)}), bf16[8,32,2048]{2,1,0:T(8,128)(2,1)}, u32[]{:S(2)}, u32[]{:S(2)}) async-start(bf16[8,32,2048]{2,1,0:T(8,128)(2,1)} %bitcast.57), calls=%async_computation.3 | async-start | bytes 2097152 | tf_op jit(solution)/shard_map/all_to_all | solution.py:77
Sparse Core Ops, SparseCore 0:
  71.0 62.3 reduce-scatter.4
  136.2 60.2 reduce-scatter.2
where the time goes:
time: 205 us; the launch traced here: 203 us
  waiting for transfers between devices  104 us (51%)
  starting transfers between devices  21.2 us (10%)
  matrix products  19.1 us (9%)
  blocking collectives  18.4 us (9%)
  local copies, waits for them, and re-layouts  17.8 us (9%)
  between operations  14.1 us (7%)
  other arithmetic  8.82 us (4%)
    reduce_scatter x1, waiting for transfers between devices, per_device(): lax.psum_scatter(contract_rows(pre_grad, inputs).astype(jnp.bfloat16), 'd...  63.2 us
    reduce_scatter x1, waiting for transfers between devices, sum_down(): lax.psum_scatter(contract_rows(hidden, scaled).astype(jnp.bfloat16), 'dp'...  19.6 us
    all_to_all x1, blocking collectives, per_device(): lax.all_to_all(sent, 'expert', split_axis=0, concat_axis=0, tiled=True)  18.4 us
    all_to_all x1, waiting for transfers between devices, per_device(): lax.all_to_all(input_grad.reshape(experts, capacity, width), 'expert', sp...  10 us
    all_to_all x1, waiting for transfers between devices, per_device(): lax.all_to_all(grads_sent, 'expert', split_axis=0, concat_axis=0, tiled=T...  8.68 us
    dot_general x2, matrix products, contract_rows(): lax.dot_general(left, right, (((0,), (0,)), ((), ())), preferred_element_...  6.59 us
    all_to_all x1, starting transfers between devices, per_device(): lax.all_to_all(prob_slots.reshape(experts, capacity), 'expert', split_axi...  6.21 us
    all_to_all x1, starting transfers between devices, per_device(): lax.all_to_all(grads_sent, 'expert', split_axis=0, concat_axis=0, tiled=T...  5.34 us
  transfers between devices with their start and end apart: 6, of which 5 were waited for; matrix products, arithmetic and copies ran while one was open for 17% of the time, Pallas kernels for 0%

commit v1 on v0

v1 whole, which is shorter than its diff:
```python
import functools

import jax
import jax.numpy as jnp
from jax import lax
from jax.experimental import pallas as pl
from jax.experimental.pallas import tpu as pltpu
from jax.sharding import PartitionSpec as P

MESH = pl.DeviceIdType.MESH
BF16, F32 = jnp.bfloat16, jnp.float32
LANES = 128


def kernel(
    n_dp, n_exp, cap, pieces,
    ids_ref, tokens_ref, weights_ref, grads_ref, gate_hbm, down_hbm,
    token_out, route_out, gate_out, down_out,
    sent, got, gate, down, preact, hid_t, da_t, back, returned, right_buf, left_buf,
    load_sem, send_sem, recv_sem, back_send, back_recv, r_send, r_recv, l_send, l_recv,
):
    rows, width = tokens_ref.shape
    slots = n_exp * cap
    units = gate.shape[0]
    part = units // n_dp
    piece = width // pieces
    tile = 256 if units % 256 == 0 else part
    r = lax.axis_index("dp")
    me = lax.axis_index("expert")

    def peer(k):
        return lax.rem(me + k, n_exp)

    def block(e):
        return pl.ds(pl.multiple_of(e * cap, cap), cap)

    loads = [
        pltpu.make_async_copy(gate_hbm, gate, load_sem.at[0]),
        pltpu.make_async_copy(down_hbm, down, load_sem.at[1]),
    ]
    for load in loads:
        load.start()

    barrier = pltpu.get_barrier_semaphore()

    @pl.loop(1, n_exp)
    def _(k):
        pl.semaphore_signal(barrier, inc=1, device_id={"expert": peer(k)}, device_id_type=MESH)

    up, low = lax.rem(r + 1, n_dp), lax.rem(r + n_dp - 1, n_dp)
    for other in (up, low):
        pl.semaphore_signal(barrier, inc=1, device_id={"dp": other}, device_id_type=MESH)

    ids = ids_ref[...]
    names = lax.broadcasted_iota(jnp.int32, (max(n_exp, 16), rows), 0)
    one_hot = (names == ids).astype(F32)
    before = (
        lax.broadcasted_iota(jnp.int32, (rows, rows), 0)
        < lax.broadcasted_iota(jnp.int32, (rows, rows), 1)
    ).astype(F32)
    counts = jnp.dot(one_hot.astype(BF16), before.astype(BF16), preferred_element_type=F32)
    rank = jnp.sum(counts * one_hot, axis=0, keepdims=True).astype(jnp.int32)
    target = ids * cap + rank
    place = (lax.broadcasted_iota(jnp.int32, (slots, rows), 0) == target).astype(F32).astype(BF16)

    sent[0] = jnp.dot(place, tokens_ref[...], preferred_element_type=F32).astype(BF16)
    pl.semaphore_wait(barrier, n_exp - 1 + 2)

    def exchange(t, k):
        to = peer(k)
        return pltpu.make_async_remote_copy(
            src_ref=sent.at[t, block(to)],
            dst_ref=got.at[t, block(me)],
            send_sem=send_sem.at[t, to],
            recv_sem=recv_sem.at[t, me],
            device_id={"expert": to},
            device_id_type=MESH,
        )

    def arrival(t, k):
        of = peer(k)
        return pltpu.make_async_remote_copy(
            src_ref=sent.at[t, block(of)],
            dst_ref=got.at[t, block(of)],
            send_sem=send_sem.at[t, of],
            recv_sem=recv_sem.at[t, of],
            device_id={"expert": of},
            device_id_type=MESH,
        )

    @pl.loop(1, n_exp)
    def _(k):
        exchange(0, k).start()

    got[0, block(me)] = sent[0, block(me)]
    weights = weights_ref[...].astype(F32)
    scaled = (weights * grads_ref[...].astype(F32)).astype(BF16)
    sent[1] = jnp.dot(place, scaled, preferred_element_type=F32).astype(BF16)

    @pl.loop(1, n_exp)
    def _(k):
        exchange(1, k).start()

    got[1, block(me)] = sent[1, block(me)]

    for load in loads:
        load.wait()

    @pl.loop(1, n_exp)
    def _(k):
        arrival(0, k).wait_recv()

    nt = (((1,), (1,)), ((), ()))

    @pl.loop(0, units // tile)
    def _(j):
        span = pl.ds(pl.multiple_of(j * tile, tile), tile)
        preact[span, :] = lax.dot_general(gate[span, :], got[0], nt, preferred_element_type=F32)

    @pl.loop(1, n_exp)
    def _(k):
        arrival(1, k).wait_recv()

    def second(j, total):
        span = pl.ds(pl.multiple_of(j * tile, tile), tile)
        slope = lax.dot_general(down[span, :], got[1], nt, preferred_element_type=F32)
        value = preact[span, :]
        sigma = jax.nn.sigmoid(value)
        hidden = (value * sigma).astype(BF16)
        hid_t[span, :] = hidden
        da_t[span, :] = (slope * (sigma * (1.0 + value * (1.0 - sigma)))).astype(BF16)
        return total + jnp.sum(hidden.astype(F32) * slope, axis=0, keepdims=True)

    route = lax.fori_loop(0, units // tile, second, jnp.zeros((1, slots), F32))

    def term(t, d, span):
        left = da_t if t == 0 else hid_t
        start = d * part if isinstance(d, int) else pl.multiple_of(d * part, part)
        return jnp.dot(
            left[pl.ds(start, part), :], got[t, :, span], preferred_element_type=F32
        )

    def columns(c):
        return pl.ds(pl.multiple_of(c * piece, piece), piece)

    def hop(buf, s_sem, r_sem, t, d, c, to):
        return pltpu.make_async_remote_copy(
            src_ref=buf.at[t, d, c],
            dst_ref=buf.at[t, d, c],
            send_sem=s_sem.at[t, d, c],
            recv_sem=r_sem.at[t, d, c],
            device_id={"dp": to},
            device_id_type=MESH,
        )

    def rightward(t, d, c, to=None):
        return hop(right_buf, r_send, r_recv, t, d - 1, c, up)

    def leftward(t, d, c, to=None):
        return hop(left_buf, l_send, l_recv, t, d, c, low)

    def pass_on(t, d, c, copy, buf, index, first):
        own = term(t, d, columns(c))

        @pl.when(first)
        def _():
            buf[t, index, c] = own.astype(BF16)

        @pl.when(jnp.logical_not(first))
        def _():
            copy.wait_recv()
            buf[t, index, c] = (own + buf[t, index, c].astype(F32)).astype(BF16)

        copy.start()

    def returning(k):
        to = peer(k)
        return pltpu.make_async_remote_copy(
            src_ref=back.at[block(to)],
            dst_ref=returned.at[block(me)],
            send_sem=back_send.at[to],
            recv_sem=back_recv.at[me],
            device_id={"expert": to},
            device_id_type=MESH,
        )

    def homecoming(k):
        of = peer(k)
        return pltpu.make_async_remote_copy(
            src_ref=back.at[block(of)],
            dst_ref=returned.at[block(of)],
            send_sem=back_send.at[of],
            recv_sem=back_recv.at[of],
            device_id={"expert": of},
            device_id_type=MESH,
        )

    def send_back():
        tn = (((0,), (0,)), ((), ()))

        @pl.loop(0, pieces)
        def _(c):
            span = columns(c)
            back[:, span] = lax.dot_general(
                da_t[...], gate[:, span], tn, preferred_element_type=F32
            ).astype(BF16)

        tall = jnp.transpose(jnp.broadcast_to(route, (LANES, slots)))
        high = tall.astype(BF16)
        rest = (tall - high.astype(F32)).astype(BF16)
        lane = lax.broadcasted_iota(jnp.int32, (slots, LANES), 1)
        back[:, pl.ds(width, LANES)] = jnp.where(
            lane < 1, high.astype(F32), rest.astype(F32)
        ).astype(BF16)

        @pl.loop(1, n_exp)
        def _(k):
            returning(k).start()

        returned[block(me), :] = back[block(me), :]

    for i in range(n_dp - 1):
        to_r, to_l = n_dp - 1 - i, i
        for t in range(2):

            @pl.loop(0, pieces)
            def _(c):
                @pl.when(r < to_r)
                def _():
                    pass_on(t, to_r, c, rightward(t, to_r, c), right_buf, to_r - 1, r == 0)

                @pl.when(r > to_l)
                def _():
                    pass_on(t, to_l, c, leftward(t, to_l, c), left_buf, to_l, r == n_dp - 1)

            if i == 0 and t == 0:
                send_back()

    @pl.loop(1, n_exp)
    def _(k):
        homecoming(k).wait_recv()

    tn = (((0,), (0,)), ((), ()))

    @pl.loop(0, pieces)
    def _(c):
        span = columns(c)
        token_out[:, span] = lax.dot_general(
            place, returned[:, span], tn, preferred_element_type=F32
        ).astype(BF16)

    pair = lax.dot_general(
        place, returned[:, pl.ds(width, LANES)], tn, preferred_element_type=F32
    )
    route_out[...] = ((pair[:, 0:1] + pair[:, 1:2]) / weights).astype(BF16)

    for t in range(2):
        out = gate_out if t == 0 else down_out

        @pl.loop(0, pieces)
        def _(c):
            span = columns(c)
            own = term(t, r, span)

            @pl.when(r == 0)
            def _():
                hop(left_buf, l_send, l_recv, t, r, c, low).wait_recv()
                out[:, span] = (own + left_buf[t, r, c].astype(F32)).astype(BF16)

            @pl.when(r == n_dp - 1)
            def _():
                hop(right_buf, r_send, r_recv, t, r - 1, c, up).wait_recv()
                out[:, span] = (own + right_buf[t, r - 1, c].astype(F32)).astype(BF16)

            @pl.when(jnp.logical_and(r > 0, r < n_dp - 1))
            def _():
                hop(left_buf, l_send, l_recv, t, r, c, low).wait_recv()
                hop(right_buf, r_send, r_recv, t, r - 1, c, up).wait_recv()
                out[:, span] = (
                    own + left_buf[t, r, c].astype(F32) + right_buf[t, r - 1, c].astype(F32)
                ).astype(BF16)

    @pl.loop(1, n_exp)
    def _(k):
        exchange(0, k).wait_send()
        exchange(1, k).wait_send()
        returning(k).wait_send()

    for i in range(n_dp - 1):
        to_r, to_l = n_dp - 1 - i, i

        @pl.loop(0, 2 * pieces)
        def _(m):
            t, c = m // pieces, lax.rem(m, pieces)

            @pl.when(r < to_r)
            def _():
                rightward(t, to_r, c).wait_send()

            @pl.when(r > to_l)
            def _():
                leftward(t, to_l, c).wait_send()


def per_device(tokens, expert_ids, route_weights, out_grad, gate_weight, down_weight):
    rows, width = tokens.shape
    n_exp, n_dp = lax.axis_size("expert"), lax.axis_size("dp")
    top = expert_ids.shape[1]
    assert top == 1
    cap = -(-max(2, 2 * rows * top // n_exp) // 16) * 16
    slots = n_exp * cap
    units = gate_weight.shape[1]
    part = units // n_dp
    pieces = max(1, width // 512)
    piece = width // pieces
    vmem = pl.BlockSpec(memory_space=pltpu.VMEM)
    hbm = pl.BlockSpec(memory_space=pl.ANY)
    token_grad, route_grad, gate_grad, down_grad = pl.pallas_call(
        functools.partial(kernel, n_dp, n_exp, cap, pieces),
        out_shape=(
            jax.ShapeDtypeStruct((rows, width), BF16),
            jax.ShapeDtypeStruct((rows, 1), BF16),
            jax.ShapeDtypeStruct((part, width), BF16),
            jax.ShapeDtypeStruct((part, width), BF16),
        ),
        in_specs=[vmem, vmem, vmem, vmem, hbm, hbm],
        out_specs=(vmem, vmem, vmem, vmem),
        scratch_shapes=[
            pltpu.VMEM((2, slots, width), BF16),
            pltpu.VMEM((2, slots, width), BF16),
            pltpu.VMEM((units, width), BF16),
            pltpu.VMEM((units, width), BF16),
            pltpu.VMEM((units, slots), F32),
            pltpu.VMEM((units, slots), BF16),
            pltpu.VMEM((units, slots), BF16),
            pltpu.VMEM((slots, width + LANES), BF16),
            pltpu.VMEM((slots, width + LANES), BF16),
            pltpu.VMEM((2, n_dp - 1, pieces, part, piece), BF16),
            pltpu.VMEM((2, n_dp - 1, pieces, part, piece), BF16),
            pltpu.SemaphoreType.DMA((2,)),
            pltpu.SemaphoreType.DMA((2, n_exp)),
            pltpu.SemaphoreType.DMA((2, n_exp)),
            pltpu.SemaphoreType.DMA((n_exp,)),
            pltpu.SemaphoreType.DMA((n_exp,)),
            pltpu.SemaphoreType.DMA((2, n_dp - 1, pieces)),
            pltpu.SemaphoreType.DMA((2, n_dp - 1, pieces)),
            pltpu.SemaphoreType.DMA((2, n_dp - 1, pieces)),
            pltpu.SemaphoreType.DMA((2, n_dp - 1, pieces)),
        ],
        compiler_params=pltpu.CompilerParams(
            collective_id=0, has_side_effects=True, vmem_limit_bytes=67_000_000
        ),
    )(
        expert_ids.reshape(1, rows), tokens, route_weights, out_grad,
        gate_weight[0], down_weight[0],
    )
    return token_grad, route_grad, gate_grad[None], down_grad[None]


def solution(mesh):
    placed = (
        P(("dp", "expert"), None),
        P(("dp", "expert"), None),
        P(("dp", "expert"), None),
        P(("dp", "expert"), None),
        P("expert", None, None),
        P("expert", None, None),
    )
    return jax.shard_map(
        per_device,
        mesh=mesh,
        in_specs=placed,
        out_specs=(
            P(("dp", "expert"), None),
            P(("dp", "expert"), None),
            P("expert", "dp", None),
            P("expert", "dp", None),
        ),
        check_vma=False,
    )
```

time: 205 us -> 163 us (0.80)
  the two profiles are of different devices: /device:TPU:1 before, /device:TPU:8 now
where the time goes in v1:
time: 163 us; the launch traced here: 162 us
  Pallas kernels  154 us (94%)
  local copies, waits for them, and re-layouts  7.66 us (5%)
    pallas_call x1, Pallas kernels, per_device(): pl.pallas_call(functools.partial(kernel, n_dp, n_exp, cap, pieces), out_s...  154 us
    unnamed x7, local copies, waits for them, and re-layouts  7.66 us

profile of v1, /device:TPU:8, one launch (start us, length us, event | category | flops | bytes accessed | tf_op | source)
XLA Modules:
  0.0 162.5 jit_solution(14057259420729377927)
XLA Ops:
  0.6 1.4 copy.10.weights_ref
  2.0 154.1 %shard_map.93 = (bf16[128,2048]{1,0:T(8,128)(2,1)}, bf16[128,1]{1,0:T(8,128)(2,1)}, bf16[192,2048]{1,0:T(8,128)(2,1)}, bf16[192,2048]{1,0:T(8,128)(2,1)}) custom-call(s32[1,128]{1,0:T(1,128)} %bitcast.9, bf16[128,2048]{1,0:T(8,128)(2,1)} %tokens_ref.1, bf16[128,1]{1,0:T(8,128)(2,1)} %copy.10.weights_ref, bf16[128,2048]{1,0:T(8,128)(2,1)} %grads_ref.1, ...), custom_call_target="tpu_custom_call" | custom-call | tf_op jit(solution)/shard_map/pallas_call | solution.py:318
  156.2 0.0 copy-start
  156.2 1.4 copy.11
  157.6 1.9 %copy.15 = bf16[128,2048]{1,0:T(8,128)(2,1)} copy(bf16[128,2048]{1,0:T(8,128)(2,1)} %get-tuple-element.20) | data formatting | bytes 1048576
  159.5 2.1 %copy.16 = bf16[1,192,2048]{2,1,0:T(8,128)(2,1)} copy(bf16[1,192,2048]{2,1,0:T(8,128)(2,1)} %bitcast.8) | data formatting | bytes 1572864
  161.6 0.0 copy-done
  161.6 0.9 copy.17
Async XLA Ops:
  156.2 5.4 %copy-start = (bf16[192,2048]{1,0:T(8,128)(2,1)S(1)}, bf16[192,2048]{1,0:T(8,128)(2,1)}, u32[]{:S(2)}) copy-start(bf16[192,2048]{1,0:T(8,128)(2,1)} %get-tuple-element.11) | copy-start | bytes 2359300

commit v2 on v1

--- a/solution.py
+++ b/solution.py
@@ -18,6 +18,7 @@
     token_out, route_out, gate_out, down_out,
     sent, got, gate, down, preact, hid_t, da_t, back, returned, right_buf, left_buf,
     load_sem, send_sem, recv_sem, back_send, back_recv, r_send, r_recv, l_send, l_recv,
+    x_send, x_recv, g_send, g_recv, cut_send, cut_recv,
 ):
     rows, width = tokens_ref.shape
     slots = n_exp * cap
@@ -93,7 +94,9 @@
         exchange(0, k).start()
 
     got[0, block(me)] = sent[0, block(me)]
-    weights = weights_ref[...].astype(F32)
+    weights = jnp.transpose(
+        jnp.broadcast_to(weights_ref[...].astype(F32), (LANES, rows))
+    )[:, 0:1]
     scaled = (weights * grads_ref[...].astype(F32)).astype(BF16)
     sent[1] = jnp.dot(place, scaled, preferred_element_type=F32).astype(BF16)
 
@@ -106,16 +109,63 @@
     for load in loads:
         load.wait()
 
+    end = jnp.logical_or(r == 0, r == n_dp - 1)
+    after_end = jnp.logical_or(r == 1, r == n_dp - 2)
+    inner = jnp.where(r == 0, up, low)
+    lower = r < n_dp // 2
+
+    def hand_x(e):
+        return pltpu.make_async_remote_copy(
+            src_ref=got.at[0, block(e)],
+            dst_ref=got.at[0, pl.ds(pl.multiple_of(slots + e * cap, cap), cap)],
+            send_sem=x_send.at[e],
+            recv_sem=x_recv.at[e],
+            device_id={"dp": inner},
+            device_id_type=MESH,
+        )
+
+    def hand_g(c):
+        span = pl.ds(pl.multiple_of(c * piece, piece), piece)
+        return pltpu.make_async_remote_copy(
+            src_ref=got.at[1, pl.ds(0, slots), span],
+            dst_ref=got.at[1, pl.ds(slots, slots), span],
+            send_sem=g_send.at[c],
+            recv_sem=g_recv.at[c],
+            device_id={"dp": inner},
+            device_id_type=MESH,
+        )
+
+    def hand_cut(t, d):
+        left = da_t if t == 0 else hid_t
+        own = pl.ds(pl.multiple_of(d * part, part), part)
+        return pltpu.make_async_remote_copy(
+            src_ref=left.at[own, pl.ds(0, slots)],
+            dst_ref=left.at[own, pl.ds(slots, slots)],
+            send_sem=cut_send.at[t, d],
+            recv_sem=cut_recv.at[t, d],
+            device_id={"dp": inner},
+            device_id_type=MESH,
+        )
+
+    @pl.when(end)
+    def _():
+        hand_x(me).start()
+
     @pl.loop(1, n_exp)
     def _(k):
         arrival(0, k).wait_recv()
+
+        @pl.when(end)
+        def _():
+            hand_x(peer(k)).start()
 
     nt = (((1,), (1,)), ((), ()))
 
     @pl.loop(0, units // tile)
     def _(j):
         span = pl.ds(pl.multiple_of(j * tile, tile), tile)
-        preact[span, :] = lax.dot_general(gate[span, :], got[0], nt, preferred_element_type=F32)
+        preact[span, :] = lax.dot_general(
+            gate[span, :], got[0, 0:slots, :], nt, preferred_element_type=F32)
 
     @pl.loop(1, n_exp)
     def _(k):
@@ -123,21 +173,38 @@
 
     def second(j, total):
         span = pl.ds(pl.multiple_of(j * tile, tile), tile)
-        slope = lax.dot_general(down[span, :], got[1], nt, preferred_element_type=F32)
+        slope = lax.dot_general(
+            down[span, :], got[1, 0:slots, :], nt, preferred_element_type=F32
+        )
         value = preact[span, :]
         sigma = jax.nn.sigmoid(value)
         hidden = (value * sigma).astype(BF16)
-        hid_t[span, :] = hidden
-        da_t[span, :] = (slope * (sigma * (1.0 + value * (1.0 - sigma)))).astype(BF16)
+        hid_t[span, 0:slots] = hidden
+        da_t[span, 0:slots] = (slope * (sigma * (1.0 + value * (1.0 - sigma)))).astype(BF16)
         return total + jnp.sum(hidden.astype(F32) * slope, axis=0, keepdims=True)
 
     route = lax.fori_loop(0, units // tile, second, jnp.zeros((1, slots), F32))
 
-    def term(t, d, span):
+    @pl.when(end)
+    def _():
+        for t in range(2):
+
+            @pl.loop(0, n_dp - 1)
+            def _(j):
+                hand_cut(t, jnp.where(r == 0, n_dp - 1 - j, j)).start()
+
+        @pl.loop(0, pieces)
+        def _(c):
+            hand_g(c).start()
+
+    def term(t, d, span, wide):
         left = da_t if t == 0 else hid_t
         start = d * part if isinstance(d, int) else pl.multiple_of(d * part, part)
+        depth = 2 * slots if wide else slots
         return jnp.dot(
-            left[pl.ds(start, part), :], got[t, :, span], preferred_element_type=F32
+            left[pl.ds(start, part), 0:depth],
+            got[t, 0:depth, span],
+            preferred_element_type=F32,
         )
 
     def columns(c):
@@ -160,18 +227,55 @@
         return hop(left_buf, l_send, l_recv, t, d, c, low)
 
     def pass_on(t, d, c, copy, buf, index, first):
-        own = term(t, d, columns(c))
-
         @pl.when(first)
         def _():
-            buf[t, index, c] = own.astype(BF16)
+            buf[t, index, c] = term(t, d, columns(c), True).astype(BF16)
 
         @pl.when(jnp.logical_not(first))
         def _():
+            own = term(t, d, columns(c), False)
             copy.wait_recv()
             buf[t, index, c] = (own + buf[t, index, c].astype(F32)).astype(BF16)
 
         copy.start()
+
+    def go_right(t):
+        for d in range(n_dp - 1, 1, -1):
+
+            @pl.when(r == 1)
+            def _():
+                hand_cut(t, d).wait_recv()
+
+            @pl.when(jnp.logical_and(r > 0, r < d))
+            def _():
+                @pl.loop(0, pieces)
+                def _(c):
+                    if t == 1 and d == n_dp - 1:
+
+                        @pl.when(r == 1)
+                        def _():
+                            hand_g(c).wait_recv()
+
+                    pass_on(t, d, c, rightward(t, d, c), right_buf, d - 1, r == 1)
+
+    def go_left(t):
+        for d in range(n_dp - 2):
+
+            @pl.when(r == n_dp - 2)
+            def _():
+                hand_cut(t, d).wait_recv()
+
+            @pl.when(jnp.logical_and(r < n_dp - 1, r > d))
+            def _():
+                @pl.loop(0, pieces)
+                def _(c):
+                    if t == 1 and d == 0:
+
+                        @pl.when(r == n_dp - 2)
+                        def _():
+                            hand_g(c).wait_recv()
+
+                    pass_on(t, d, c, leftward(t, d, c), left_buf, d, r == n_dp - 2)
 
     def returning(k):
         to = peer(k)
@@ -202,7 +306,7 @@
         def _(c):
             span = columns(c)
             back[:, span] = lax.dot_general(
-                da_t[...], gate[:, span], tn, preferred_element_type=F32
+                da_t[:, 0:slots], gate[:, span], tn, preferred_element_type=F32
             ).astype(BF16)
 
         tall = jnp.transpose(jnp.broadcast_to(route, (LANES, slots)))
@@ -219,22 +323,25 @@
 
         returned[block(me), :] = back[block(me), :]
 
-    for i in range(n_dp - 1):
-        to_r, to_l = n_dp - 1 - i, i
-        for t in range(2):
-
-            @pl.loop(0, pieces)
-            def _(c):
-                @pl.when(r < to_r)
-                def _():
-                    pass_on(t, to_r, c, rightward(t, to_r, c), right_buf, to_r - 1, r == 0)
-
-                @pl.when(r > to_l)
-                def _():
-                    pass_on(t, to_l, c, leftward(t, to_l, c), left_buf, to_l, r == n_dp - 1)
-
-            if i == 0 and t == 0:
-                send_back()
+    send_back()
+
+    @pl.when(after_end)
+    def _():
+        @pl.loop(0, n_exp)
+        def _(e):
+            hand_x(e).wait_recv()
+
+    for t in range(2):
+
+        @pl.when(lower)
+        def _():
+            go_right(t)
+
+        go_left(t)
+
+        @pl.when(jnp.logical_not(lower))
+        def _():
+            go_right(t)
 
     @pl.loop(1, n_exp)
     def _(k):
@@ -252,33 +359,47 @@
     pair = lax.dot_general(
         place, returned[:, pl.ds(width, LANES)], tn, preferred_element_type=F32
     )
-    route_out[...] = ((pair[:, 0:1] + pair[:, 1:2]) / weights).astype(BF16)
+    total = jnp.broadcast_to((pair[:, 0:1] + pair[:, 1:2]) / weights, (rows, LANES))
+    route_out[...] = jnp.transpose(total)[0:1, :].astype(BF16)
 
     for t in range(2):
         out = gate_out if t == 0 else down_out
+
+        @pl.when(after_end)
+        def _():
+            hand_cut(t, r).wait_recv()
 
         @pl.loop(0, pieces)
         def _(c):
             span = columns(c)
-            own = term(t, r, span)
+
+            def from_right():
+                hop(left_buf, l_send, l_recv, t, r, c, low).wait_recv()
+                return left_buf[t, r, c].astype(F32)
+
+            def from_left():
+                hop(right_buf, r_send, r_recv, t, r - 1, c, up).wait_recv()
+                return right_buf[t, r - 1, c].astype(F32)
 
             @pl.when(r == 0)
             def _():
-                hop(left_buf, l_send, l_recv, t, r, c, low).wait_recv()
-                out[:, span] = (own + left_buf[t, r, c].astype(F32)).astype(BF16)
+                out[:, span] = (term(t, r, span, False) + from_right()).astype(BF16)
 
             @pl.when(r == n_dp - 1)
             def _():
-                hop(right_buf, r_send, r_recv, t, r - 1, c, up).wait_recv()
-                out[:, span] = (own + right_buf[t, r - 1, c].astype(F32)).astype(BF16)
-
-            @pl.when(jnp.logical_and(r > 0, r < n_dp - 1))
-            def _():
-                hop(left_buf, l_send, l_recv, t, r, c, low).wait_recv()
-                hop(right_buf, r_send, r_recv, t, r - 1, c, up).wait_recv()
-                out[:, span] = (
-                    own + left_buf[t, r, c].astype(F32) + right_buf[t, r - 1, c].astype(F32)
-                ).astype(BF16)
+                out[:, span] = (term(t, r, span, False) + from_left()).astype(BF16)
+
+            @pl.when(r == 1)
+            def _():
+                out[:, span] = (term(t, r, span, True) + from_right()).astype(BF16)
+
+            @pl.when(r == n_dp - 2)
+            def _():
+                out[:, span] = (term(t, r, span, True) + from_left()).astype(BF16)
+
+            @pl.when(jnp.logical_and(r > 1, r < n_dp - 2))
+            def _():
+                out[:, span] = (term(t, r, span, False) + from_right() + from_left()).astype(BF16)
 
     @pl.loop(1, n_exp)
     def _(k):
@@ -286,27 +407,51 @@
         exchange(1, k).wait_send()
         returning(k).wait_send()
 
-    for i in range(n_dp - 1):
-        to_r, to_l = n_dp - 1 - i, i
-
-        @pl.loop(0, 2 * pieces)
-        def _(m):
-            t, c = m // pieces, lax.rem(m, pieces)
-
-            @pl.when(r < to_r)
-            def _():
-                rightward(t, to_r, c).wait_send()
-
-            @pl.when(r > to_l)
-            def _():
-                leftward(t, to_l, c).wait_send()
+    @pl.when(end)
+    def _():
+        @pl.loop(0, n_exp)
+        def _(e):
+            hand_x(e).wait_send()
+
+        @pl.loop(0, pieces)
+        def _(c):
+            hand_g(c).wait_send()
+
+        for t in range(2):
+
+            @pl.loop(0, n_dp - 1)
+            def _(j):
+                hand_cut(t, jnp.where(r == 0, n_dp - 1 - j, j)).wait_send()
+
+    for t in range(2):
+        for d in range(n_dp):
+
+            @pl.loop(0, pieces)
+            def _(c):
+                if d > 1:
+
+                    @pl.when(jnp.logical_and(r > 0, r < d))
+                    def _():
+                        rightward(t, d, c).wait_send()
+
+                if d < n_dp - 2:
+
+                    @pl.when(jnp.logical_and(r < n_dp - 1, r > d))
+                    def _():
+                        leftward(t, d, c).wait_send()
+
+
+def settle(*refs):
+    half = len(refs) // 2
+    for source, out in zip(refs[:half], refs[half:]):
+        out[...] = source[...]
 
 
 def per_device(tokens, expert_ids, route_weights, out_grad, gate_weight, down_weight):
     rows, width = tokens.shape
     n_exp, n_dp = lax.axis_size("expert"), lax.axis_size("dp")
     top = expert_ids.shape[1]
-    assert top == 1
+    assert top == 1 and n_dp >= 4
     cap = -(-max(2, 2 * rows * top // n_exp) // 16) * 16
     slots = n_exp * cap
     units = gate_weight.shape[1]
@@ -315,11 +460,11 @@
     piece = width // pieces
     vmem = pl.BlockSpec(memory_space=pltpu.VMEM)
     hbm = pl.BlockSpec(memory_space=pl.ANY)
-    token_grad, route_grad, gate_grad, down_grad = pl.pallas_call(
+    results = pl.pallas_call(
         functools.partial(kernel, n_dp, n_exp, cap, pieces),
         out_shape=(
             jax.ShapeDtypeStruct((rows, width), BF16),
-            jax.ShapeDtypeStruct((rows, 1), BF16),
+            jax.ShapeDtypeStruct((1, rows), BF16),
             jax.ShapeDtypeStruct((part, width), BF16),
             jax.ShapeDtypeStruct((part, width), BF16),
         ),
@@ -327,12 +472,12 @@
         out_specs=(vmem, vmem, vmem, vmem),
         scratch_shapes=[
             pltpu.VMEM((2, slots, width), BF16),
-            pltpu.VMEM((2, slots, width), BF16),
+            pltpu.VMEM((2, 2 * slots, width), BF16),
             pltpu.VMEM((units, width), BF16),
             pltpu.VMEM((units, width), BF16),
             pltpu.VMEM((units, slots), F32),
-            pltpu.VMEM((units, slots), BF16),
-            pltpu.VMEM((units, slots), BF16),
+            pltpu.VMEM((units, 2 * slots), BF16),
+            pltpu.VMEM((units, 2 * slots), BF16),
             pltpu.VMEM((slots, width + LANES), BF16),
             pltpu.VMEM((slots, width + LANES), BF16),
             pltpu.VMEM((2, n_dp - 1, pieces, part, piece), BF16),
@@ -346,15 +491,27 @@
             pltpu.SemaphoreType.DMA((2, n_dp - 1, pieces)),
             pltpu.SemaphoreType.DMA((2, n_dp - 1, pieces)),
             pltpu.SemaphoreType.DMA((2, n_dp - 1, pieces)),
+            pltpu.SemaphoreType.DMA((n_exp,)),
+            pltpu.SemaphoreType.DMA((n_exp,)),
+            pltpu.SemaphoreType.DMA((pieces,)),
+            pltpu.SemaphoreType.DMA((pieces,)),
+            pltpu.SemaphoreType.DMA((2, n_dp)),
+            pltpu.SemaphoreType.DMA((2, n_dp)),
         ],
         compiler_params=pltpu.CompilerParams(
             collective_id=0, has_side_effects=True, vmem_limit_bytes=67_000_000
         ),
     )(
-        expert_ids.reshape(1, rows), tokens, route_weights, out_grad,
+        expert_ids.reshape(1, rows), tokens, route_weights.reshape(1, rows), out_grad,
         gate_weight[0], down_weight[0],
     )
-    return token_grad, route_grad, gate_grad[None], down_grad[None]
+    token_grad, route_grad, gate_grad, down_grad = pl.pallas_call(
+        settle,
+        out_shape=tuple(jax.ShapeDtypeStruct(a.shape, a.dtype) for a in results),
+        in_specs=[vmem] * 4,
+        out_specs=(vmem,) * 4,
+    )(*results)
+    return token_grad, route_grad.reshape(rows, 1), gate_grad[None], down_grad[None]
 
 
 def solution(mesh):

time: 163 us -> 113 us (0.69)
  the two profiles are of different devices: /device:TPU:8 before, /device:TPU:11 now
where the time goes in v2:
time: 113 us; the launch traced here: 112 us
  Pallas kernels  112 us (99%)
    pallas_call x1, Pallas kernels, per_device(): pl.pallas_call(functools.partial(kernel, n_dp, n_exp, cap, pieces), out_s...  109 us
    pallas_call x1, Pallas kernels, per_device(): pl.pallas_call(settle, out_shape=tuple((jax.ShapeDtypeStruct(a.shape, a.d...  2.88 us

profile of v2, /device:TPU:11, one launch (start us, length us, event | category | flops | bytes accessed | tf_op | source)
XLA Modules:
  0.0 112.4 jit_solution(11133804260330885020)
XLA Ops:
  0.6 108.8 %shard_map.93 = (bf16[128,2048]{1,0:T(8,128)(2,1)}, bf16[1,128]{1,0:T(2,128)(2,1)}, bf16[192,2048]{1,0:T(8,128)(2,1)}, bf16[192,2048]{1,0:T(8,128)(2,1)}) custom-call(s32[1,128]{1,0:T(1,128)} %bitcast.9, bf16[128,2048]{1,0:T(8,128)(2,1)} %tokens_ref.1, bf16[1,128]{1,0:T(2,128)(2,1)} %bitcast.10, bf16[128,2048]{1,0:T(8,128)(2,1)} %grads_ref.1, ...), custom_call_target="tpu_custom_call" | custom-call | tf_op jit(solution)/shard_map/pallas_call | solution.py:463
  109.5 2.9 %shard_map.94 = (bf16[128,2048]{1,0:T(8,128)(2,1)}, bf16[1,128]{1,0:T(2,128)(2,1)}, bf16[192,2048]{1,0:T(8,128)(2,1)}, bf16[192,2048]{1,0:T(8,128)(2,1)}) custom-call(bf16[128,2048]{1,0:T(8,128)(2,1)} %get-tuple-element.12.refs_0_, bf16[1,128]{1,0:T(2,128)(2,1)} %get-tuple-element.13.refs_1_, bf16[192,2048]{1,0:T(8,128)(2,1)} %get-tuple-element.14.refs_2_, ...), custom_call_target="tpu_custom_call" | custom-call | tf_op jit(solution)/shard_map/pallas_call | solution.py:508

commit v3 on v2

--- a/solution.py
+++ b/solution.py
@@ -19,6 +19,8 @@
     sent, got, gate, down, preact, hid_t, da_t, back, returned, right_buf, left_buf,
     load_sem, send_sem, recv_sem, back_send, back_recv, r_send, r_recv, l_send, l_recv,
     x_send, x_recv, g_send, g_recv, cut_send, cut_recv,
+    raw, raw_ids, far_sent, pair_out, pair_in,
+    raw_send, raw_recv, far_send, far_recv, slice_send, slice_recv, pair_send, pair_recv,
 ):
     rows, width = tokens_ref.shape
     slots = n_exp * cap
@@ -49,23 +51,88 @@
         pl.semaphore_signal(barrier, inc=1, device_id={"expert": peer(k)}, device_id_type=MESH)
 
     up, low = lax.rem(r + 1, n_dp), lax.rem(r + n_dp - 1, n_dp)
-    for other in (up, low):
+    deep = n_dp == 4
+
+    @pl.loop(1, n_dp)
+    def _(k):
+        other = lax.rem(r + k, n_dp)
         pl.semaphore_signal(barrier, inc=1, device_id={"dp": other}, device_id_type=MESH)
 
-    ids = ids_ref[...]
-    names = lax.broadcasted_iota(jnp.int32, (max(n_exp, 16), rows), 0)
-    one_hot = (names == ids).astype(F32)
-    before = (
-        lax.broadcasted_iota(jnp.int32, (rows, rows), 0)
-        < lax.broadcasted_iota(jnp.int32, (rows, rows), 1)
-    ).astype(F32)
-    counts = jnp.dot(one_hot.astype(BF16), before.astype(BF16), preferred_element_type=F32)
-    rank = jnp.sum(counts * one_hot, axis=0, keepdims=True).astype(jnp.int32)
-    target = ids * cap + rank
-    place = (lax.broadcasted_iota(jnp.int32, (slots, rows), 0) == target).astype(F32).astype(BF16)
+    def placement(ids):
+        names = lax.broadcasted_iota(jnp.int32, (max(n_exp, 16), rows), 0)
+        one_hot = (names == ids).astype(F32)
+        before = (
+            lax.broadcasted_iota(jnp.int32, (rows, rows), 0)
+            < lax.broadcasted_iota(jnp.int32, (rows, rows), 1)
+        ).astype(F32)
+        counts = jnp.dot(one_hot.astype(BF16), before.astype(BF16), preferred_element_type=F32)
+        rank = jnp.sum(counts * one_hot, axis=0, keepdims=True).astype(jnp.int32)
+        target = ids * cap + rank
+        match = lax.broadcasted_iota(jnp.int32, (slots, rows), 0) == target
+        return match.astype(F32).astype(BF16)
+
+    place = placement(ids_ref[...])
+    is_end = jnp.logical_or(r == 0, r == n_dp - 1)
+    which = jnp.where(is_end, 0, 1)
+    across = jnp.where(r < 2, 2, 1)
+
+    def raw_copies(j):
+        return [
+            pltpu.make_async_remote_copy(
+                src_ref=source, dst_ref=held.at[j],
+                send_sem=raw_send.at[i], recv_sem=raw_recv.at[i, j],
+                device_id={"dp": across}, device_id_type=MESH,
+            )
+            for i, (source, held) in enumerate(((ids_ref, raw_ids), (tokens_ref, raw)))
+        ]
+
+    def far_block(j, e):
+        return pl.ds(pl.multiple_of((1 + j) * slots + e * cap, cap), cap)
+
+    def far_exchange(j, to, at, peer_id=None):
+        return pltpu.make_async_remote_copy(
+            src_ref=far_sent.at[j, block(to)],
+            dst_ref=got.at[0, far_block(j, at)],
+            send_sem=far_send.at[j, to],
+            recv_sem=far_recv.at[j, at],
+            device_id={"expert": to if peer_id is None else peer_id},
+            device_id_type=MESH,
+        )
+
+    def slice_copy(j):
+        own = pl.ds(pl.multiple_of(jnp.where(r < 2, 2 * part, 0), part), 2 * part)
+        return pltpu.make_async_remote_copy(
+            src_ref=da_t.at[own, pl.ds(0, slots)],
+            dst_ref=da_t.at[own, pl.ds(pl.multiple_of((1 + j) * slots, slots), slots)],
+            send_sem=slice_send,
+            recv_sem=slice_recv.at[j],
+            device_id={"dp": across},
+            device_id_type=MESH,
+        )
+
+    def slice_wait(j):
+        own = pl.ds(pl.multiple_of(jnp.where(r < 2, 0, 2 * part), part), 2 * part)
+        far = pl.ds(pl.multiple_of((1 + j) * slots, slots), slots)
+        return pltpu.make_async_remote_copy(
+            src_ref=da_t.at[own, pl.ds(0, slots)],
+            dst_ref=da_t.at[own, far],
+            send_sem=slice_send,
+            recv_sem=slice_recv.at[j],
+            device_id={"dp": across},
+            device_id_type=MESH,
+        )
+
+    partner = r + 1 - 2 * lax.rem(r, 2)
+
+    def pair_copy(c):
+        return pltpu.make_async_remote_copy(
+            src_ref=pair_out.at[c], dst_ref=pair_in.at[c],
+            send_sem=pair_send.at[c], recv_sem=pair_recv.at[c],
+            device_id={"dp": partner}, device_id_type=MESH,
+        )
 
     sent[0] = jnp.dot(place, tokens_ref[...], preferred_element_type=F32).astype(BF16)
-    pl.semaphore_wait(barrier, n_exp - 1 + 2)
+    pl.semaphore_wait(barrier, n_exp - 1 + n_dp - 1)
 
     def exchange(t, k):
         to = peer(k)
@@ -92,6 +159,10 @@
     @pl.loop(1, n_exp)
     def _(k):
         exchange(0, k).start()
+
+    if deep:
+        for copy in raw_copies(which):
+            copy.start()
 
     got[0, block(me)] = sent[0, block(me)]
     weights = jnp.transpose(
@@ -116,8 +187,8 @@
 
     def hand_x(e):
         return pltpu.make_async_remote_copy(
-            src_ref=got.at[0, block(e)],
-            dst_ref=got.at[0, pl.ds(pl.multiple_of(slots + e * cap, cap), cap)],
+            src_ref=got.at[first, block(e)],
+            dst_ref=got.at[first, pl.ds(pl.multiple_of(slots + e * cap, cap), cap)],
             send_sem=x_send.at[e],
             recv_sem=x_recv.at[e],
             device_id={"dp": inner},
@@ -147,6 +218,8 @@
             device_id_type=MESH,
         )
 
+    first = 1 if deep else 0
+
     @pl.when(end)
     def _():
         hand_x(me).start()
@@ -155,21 +228,42 @@
     def _(k):
         arrival(0, k).wait_recv()
 
-        @pl.when(end)
-        def _():
-            hand_x(peer(k)).start()
+        if not deep:
+
+            @pl.when(end)
+            def _():
+                hand_x(peer(k)).start()
 
     nt = (((1,), (1,)), ((), ()))
 
     @pl.loop(0, units // tile)
     def _(j):
         span = pl.ds(pl.multiple_of(j * tile, tile), tile)
-        preact[span, :] = lax.dot_general(
-            gate[span, :], got[0, 0:slots, :], nt, preferred_element_type=F32)
+        value = lax.dot_general(
+            gate[span, :], got[0, 0:slots, :], nt, preferred_element_type=F32
+        )
+        preact[span, :] = value
+        hid_t[span, 0:slots] = (value * jax.nn.sigmoid(value)).astype(BF16)
+
+    def hand_cuts(t):
+        @pl.when(end)
+        def _():
+            @pl.loop(0, n_dp - 1)
+            def _(j):
+                hand_cut(t, jnp.where(r == 0, n_dp - 1 - j, j)).start()
+
+    if deep:
+        hand_cuts(1)
 
     @pl.loop(1, n_exp)
     def _(k):
         arrival(1, k).wait_recv()
+
+        if deep:
+
+            @pl.when(end)
+            def _():
+                hand_x(peer(k)).start()
 
     def second(j, total):
         span = pl.ds(pl.multiple_of(j * tile, tile), tile)
@@ -178,29 +272,42 @@
         )
         value = preact[span, :]
         sigma = jax.nn.sigmoid(value)
-        hidden = (value * sigma).astype(BF16)
-        hid_t[span, 0:slots] = hidden
         da_t[span, 0:slots] = (slope * (sigma * (1.0 + value * (1.0 - sigma)))).astype(BF16)
-        return total + jnp.sum(hidden.astype(F32) * slope, axis=0, keepdims=True)
+        return total + jnp.sum(hid_t[span, 0:slots].astype(F32) * slope, axis=0, keepdims=True)
 
     route = lax.fori_loop(0, units // tile, second, jnp.zeros((1, slots), F32))
 
-    @pl.when(end)
-    def _():
-        for t in range(2):
-
-            @pl.loop(0, n_dp - 1)
-            def _(j):
-                hand_cut(t, jnp.where(r == 0, n_dp - 1 - j, j)).start()
-
-        @pl.loop(0, pieces)
-        def _(c):
-            hand_g(c).start()
+    if deep:
+        slice_copy(which).start()
+
+        @pl.when(after_end)
+        def _():
+            for j in (1, 0):
+                for copy in raw_copies(j):
+                    copy.wait_recv()
+                far_sent[j] = jnp.dot(
+                    placement(raw_ids[j]), raw[j], preferred_element_type=F32
+                ).astype(BF16)
+
+                @pl.loop(1, n_exp)
+                def _(k):
+                    far_exchange(j, peer(k), me).start()
+
+                got[0, far_block(j, me)] = far_sent[j, block(me)]
+    else:
+        hand_cuts(0)
+        hand_cuts(1)
+
+        @pl.when(end)
+        def _():
+            @pl.loop(0, pieces)
+            def _(c):
+                hand_g(c).start()
 
     def term(t, d, span, wide):
         left = da_t if t == 0 else hid_t
         start = d * part if isinstance(d, int) else pl.multiple_of(d * part, part)
-        depth = 2 * slots if wide else slots
+        depth = (3 if deep and t == 0 else 2) * slots if wide else slots
         return jnp.dot(
             left[pl.ds(start, part), 0:depth],
             got[t, 0:depth, span],
@@ -250,7 +357,7 @@
             def _():
                 @pl.loop(0, pieces)
                 def _(c):
-                    if t == 1 and d == n_dp - 1:
+                    if not deep and t == 1 and d == n_dp - 1:
 
                         @pl.when(r == 1)
                         def _():
@@ -269,7 +376,7 @@
             def _():
                 @pl.loop(0, pieces)
                 def _(c):
-                    if t == 1 and d == 0:
+                    if not deep and t == 1 and d == 0:
 
                         @pl.when(r == n_dp - 2)
                         def _():
@@ -331,7 +438,7 @@
         def _(e):
             hand_x(e).wait_recv()
 
-    for t in range(2):
+    for t in range(first, 2):
 
         @pl.when(lower)
         def _():
@@ -342,6 +449,27 @@
         @pl.when(jnp.logical_not(lower))
         def _():
             go_right(t)
+
+    if deep:
+
+        @pl.when(after_end)
+        def _():
+            for j in (1, 0):
+                slice_wait(j).wait_recv()
+
+                @pl.loop(1, n_exp)
+                def _(k):
+                    far_exchange(j, me, peer(k), peer(k)).wait_recv()
+
+        @pl.loop(0, pieces)
+        def _(c):
+            for wide, role in ((True, after_end), (False, end)):
+
+                @pl.when(role)
+                def _():
+                    pair_out[c] = term(0, partner, columns(c), wide).astype(BF16)
+
+            pair_copy(c).start()
 
     @pl.loop(1, n_exp)
     def _(k):
@@ -362,7 +490,20 @@
     total = jnp.broadcast_to((pair[:, 0:1] + pair[:, 1:2]) / weights, (rows, LANES))
     route_out[...] = jnp.transpose(total)[0:1, :].astype(BF16)
 
-    for t in range(2):
+    if deep:
+
+        @pl.loop(0, pieces)
+        def _(c):
+            span = columns(c)
+            for wide, role in ((True, after_end), (False, end)):
+
+                @pl.when(role)
+                def _():
+                    own = term(0, r, span, wide)
+                    pair_copy(c).wait_recv()
+                    gate_out[:, span] = (own + pair_in[c].astype(F32)).astype(BF16)
+
+    for t in range(first, 2):
         out = gate_out if t == 0 else down_out
 
         @pl.when(after_end)
@@ -413,17 +554,36 @@
         def _(e):
             hand_x(e).wait_send()
 
-        @pl.loop(0, pieces)
-        def _(c):
-            hand_g(c).wait_send()
-
-        for t in range(2):
+        if not deep:
+
+            @pl.loop(0, pieces)
+            def _(c):
+                hand_g(c).wait_send()
+
+        for t in range(first, 2):
 
             @pl.loop(0, n_dp - 1)
             def _(j):
                 hand_cut(t, jnp.where(r == 0, n_dp - 1 - j, j)).wait_send()
 
-    for t in range(2):
+    if deep:
+        for copy in raw_copies(which):
+            copy.wait_send()
+        slice_copy(which).wait_send()
+
+        @pl.loop(0, pieces)
+        def _(c):
+            pair_copy(c).wait_send()
+
+        @pl.when(after_end)
+        def _():
+            for j in (1, 0):
+
+                @pl.loop(1, n_exp)
+                def _(k):
+                    far_exchange(j, peer(k), me).wait_send()
+
+    for t in range(first, 2):
         for d in range(n_dp):
 
             @pl.loop(0, pieces)
@@ -458,6 +618,8 @@
     part = units // n_dp
     pieces = max(1, width // 512)
     piece = width // pieces
+    deep = n_dp == 4
+    copies = 3 if deep else 2
     vmem = pl.BlockSpec(memory_space=pltpu.VMEM)
     hbm = pl.BlockSpec(memory_space=pl.ANY)
     results = pl.pallas_call(
@@ -472,12 +634,12 @@
         out_specs=(vmem, vmem, vmem, vmem),
         scratch_shapes=[
             pltpu.VMEM((2, slots, width), BF16),
-            pltpu.VMEM((2, 2 * slots, width), BF16),
+            pltpu.VMEM((2, copies * slots, width), BF16),
             pltpu.VMEM((units, width), BF16),
             pltpu.VMEM((units, width), BF16),
             pltpu.VMEM((units, slots), F32),
-            pltpu.VMEM((units, 2 * slots), BF16),
-            pltpu.VMEM((units, 2 * slots), BF16),
+            pltpu.VMEM((units, copies * slots), BF16),
+            pltpu.VMEM((units, copies * slots), BF16),
             pltpu.VMEM((slots, width + LANES), BF16),
             pltpu.VMEM((slots, width + LANES), BF16),
             pltpu.VMEM((2, n_dp - 1, pieces, part, piece), BF16),
@@ -497,6 +659,19 @@
             pltpu.SemaphoreType.DMA((pieces,)),
             pltpu.SemaphoreType.DMA((2, n_dp)),
             pltpu.SemaphoreType.DMA((2, n_dp)),
+            pltpu.VMEM((2, rows, width) if deep else (2, 16, LANES), BF16),
+            pltpu.VMEM((2, 1, rows), jnp.int32),
+            pltpu.VMEM((2, slots, width) if deep else (2, 16, LANES), BF16),
+            pltpu.VMEM((pieces, part, piece) if deep else (1, 16, LANES), BF16),
+            pltpu.VMEM((pieces, part, piece) if deep else (1, 16, LANES), BF16),
+            pltpu.SemaphoreType.DMA((2,)),
+            pltpu.SemaphoreType.DMA((2, 2)),
+            pltpu.SemaphoreType.DMA((2, n_exp)),
+            pltpu.SemaphoreType.DMA((2, n_exp)),
+            pltpu.SemaphoreType.DMA,
+            pltpu.SemaphoreType.DMA((2,)),
+            pltpu.SemaphoreType.DMA((pieces,)),
+            pltpu.SemaphoreType.DMA((pieces,)),
         ],
         compiler_params=pltpu.CompilerParams(
             collective_id=0, has_side_effects=True, vmem_limit_bytes=67_000_000

time: 113 us -> 100 us (0.88)
  the two profiles are of different devices: /device:TPU:11 before, /device:TPU:1 now
where the time goes in v3:
time: 100 us
  Pallas kernels  99.4 us (99%)
    pallas_call x1, Pallas kernels, per_device(): pl.pallas_call(functools.partial(kernel, n_dp, n_exp, cap, pieces), out_s...  96.5 us
    pallas_call x1, Pallas kernels, per_device(): pl.pallas_call(settle, out_shape=tuple((jax.ShapeDtypeStruct(a.shape, a.d...  2.88 us

profile of v3, /device:TPU:1, one launch (start us, length us, event | category | flops | bytes accessed | tf_op | source)
XLA Modules:
  0.0 100.0 jit_solution(4848099748898603269)
XLA Ops:
  0.6 96.5 %shard_map.93 = (bf16[128,2048]{1,0:T(8,128)(2,1)}, bf16[1,128]{1,0:T(2,128)(2,1)}, bf16[192,2048]{1,0:T(8,128)(2,1)}, bf16[192,2048]{1,0:T(8,128)(2,1)}) custom-call(s32[1,128]{1,0:T(1,128)} %bitcast.9, bf16[128,2048]{1,0:T(8,128)(2,1)} %tokens_ref.1, bf16[1,128]{1,0:T(2,128)(2,1)} %bitcast.10, bf16[128,2048]{1,0:T(8,128)(2,1)} %grads_ref.1, ...), custom_call_target="tpu_custom_call" | custom-call | tf_op jit(solution)/shard_map/pallas_call | solution.py:625
  97.1 2.9 %shard_map.94 = (bf16[128,2048]{1,0:T(8,128)(2,1)}, bf16[1,128]{1,0:T(2,128)(2,1)}, bf16[192,2048]{1,0:T(8,128)(2,1)}, bf16[192,2048]{1,0:T(8,128)(2,1)}) custom-call(bf16[128,2048]{1,0:T(8,128)(2,1)} %get-tuple-element.12.refs_0_, bf16[1,128]{1,0:T(2,128)(2,1)} %get-tuple-element.13.refs_1_, bf16[192,2048]{1,0:T(8,128)(2,1)} %get-tuple-element.14.refs_2_, ...), custom_call_target="tpu_custom_call" | custom-call | tf_op jit(solution)/shard_map/pallas_call | solution.py:683

commit v4 on v3

--- a/solution.py
+++ b/solution.py
@@ -674,7 +674,7 @@
             pltpu.SemaphoreType.DMA((pieces,)),
         ],
         compiler_params=pltpu.CompilerParams(
-            collective_id=0, has_side_effects=True, vmem_limit_bytes=67_000_000
+            collective_id=0, has_side_effects=True, vmem_limit_bytes=46_000_000 if deep else 67_000_000
         ),
     )(
         expert_ids.reshape(1, rows), tokens, route_weights.reshape(1, rows), out_grad,

time: 100 us -> 109 us (1.090)
  local copies, waits for them, and re-layouts: 0 us -> 10.3 us
  Pallas kernels: 99.4 us -> 97.3 us
    unnamed x0 -> x20, local copies, waits for them, and re-layouts: none -> 10.3 us
    pallas_call x1, Pallas kernels: 96.5 us -> 94.4 us  [per_device(): pl.pallas_call(functools.partial(kernel, n_dp, n_exp, cap, pieces), out_s...]
where the time goes in v4:
time: 109 us; the launch traced here: 108 us
  Pallas kernels  97.3 us (89%)
  local copies, waits for them, and re-layouts  10.3 us (9%)
    pallas_call x1, Pallas kernels, per_device(): pl.pallas_call(functools.partial(kernel, n_dp, n_exp, cap, pieces), out_s...  94.4 us
    unnamed x20, local copies, waits for them, and re-layouts  10.3 us
    pallas_call x1, Pallas kernels, per_device(): pl.pallas_call(settle, out_shape=tuple((jax.ShapeDtypeStruct(a.shape, a.d...  2.88 us

profile of v4, /device:TPU:1, one launch (start us, length us, event | category | flops | bytes accessed | tf_op | source)
XLA Modules:
  0.0 108.3 jit_solution(14007323737602193060)
XLA Ops:
  0.6 0.0 copy-start
  0.6 1.9 %copy-done = bf16[1,768,2048]{2,1,0:T(8,128)(2,1)S(1)} copy-done((bf16[1,768,2048]{2,1,0:T(8,128)(2,1)S(1)}, bf16[1,768,2048]{2,1,0:T(8,128)(2,1)}, u32[]{:S(2)}) %copy-start) | copy-done | bytes 3145752
  2.5 0.0 copy-start.1
  2.5 1.9 %copy-done.1 = bf16[1,768,2048]{2,1,0:T(8,128)(2,1)S(1)} copy-done((bf16[1,768,2048]{2,1,0:T(8,128)(2,1)S(1)}, bf16[1,768,2048]{2,1,0:T(8,128)(2,1)}, u32[]{:S(2)}) %copy-start.1) | copy-done | bytes 3145752
  4.4 0.0 copy-start.5
  4.4 1.0 copy-done.5
  5.5 0.0 copy-start.6
  5.5 1.0 copy-done.6
  6.5 0.0 copy-start.7
  6.5 0.7 copy-done.7
  7.2 0.0 copy-start.8
  7.2 0.7 copy-done.8
  7.8 94.4 %shard_map.93 = (bf16[128,2048]{1,0:T(8,128)(2,1)S(1)}, bf16[1,128]{1,0:T(2,128)(2,1)S(1)}, bf16[192,2048]{1,0:T(8,128)(2,1)S(1)}, bf16[192,2048]{1,0:T(8,128)(2,1)S(1)}) custom-call(s32[1,128]{1,0:T(1,128)S(1)} %bitcast.9, bf16[128,2048]{1,0:T(8,128)(2,1)S(1)} %copy-done.5, bf16[1,128]{1,0:T(2,128)(2,1)S(1)} %bitcast.10, bf16[128,2048]{1,0:T(8,128)(2,1)S(1)} %copy-done.6, ...), custom_call_target="tpu_custom_call" | custom-call | tf_op jit(solution)/shard_map/pallas_call | solution.py:625
  102.2 0.0 copy-start.2
  102.2 0.9 copy-done.2
  103.1 0.0 copy-start.3
  103.1 0.9 copy-done.3
  104.0 0.0 copy-start.4
  104.0 0.8 copy-done.4
  104.8 0.0 copy-start.9
  104.8 0.6 copy-done.9
  105.4 2.9 %shard_map.94 = (bf16[128,2048]{1,0:T(8,128)(2,1)}, bf16[1,128]{1,0:T(2,128)(2,1)}, bf16[192,2048]{1,0:T(8,128)(2,1)}, bf16[192,2048]{1,0:T(8,128)(2,1)}) custom-call(bf16[128,2048]{1,0:T(8,128)(2,1)} %copy-done.4, bf16[1,128]{1,0:T(2,128)(2,1)} %copy-done.9, bf16[192,2048]{1,0:T(8,128)(2,1)} %copy-done.2, bf16[192,2048]{1,0:T(8,128)(2,1)} %copy-done.3), custom_call_target="tpu_custom_call" | custom-call | tf_op jit(solution)/shard_map/pallas_call | solution.py:683
Async XLA Ops:
  0.6 1.9 %copy-start = (bf16[1,768,2048]{2,1,0:T(8,128)(2,1)S(1)}, bf16[1,768,2048]{2,1,0:T(8,128)(2,1)}, u32[]{:S(2)}) copy-start(bf16[1,768,2048]{2,1,0:T(8,128)(2,1)} %param.10) | copy-start | bytes 9437188
  2.5 1.9 %copy-start.1 = (bf16[1,768,2048]{2,1,0:T(8,128)(2,1)S(1)}, bf16[1,768,2048]{2,1,0:T(8,128)(2,1)}, u32[]{:S(2)}) copy-start(bf16[1,768,2048]{2,1,0:T(8,128)(2,1)} %param.11) | copy-start | bytes 9437188
  4.4 1.0 copy-start.5
  5.5 1.0 copy-start.6
  6.5 0.7 copy-start.7
  7.2 0.7 copy-start.8
  102.2 0.9 copy-start.2
  103.1 0.9 copy-start.3
  104.0 0.8 copy-start.4
  104.8 0.6 copy-start.9
